TPU v7x, 32 devices: a whole 2x2x4 slice. The times are simulated.
32 devices in a mesh: seq: 8 (over z, x), head: 4 (over y, core).
Axes of the slice: x: 2, y: 2, z: 4, core: 2. Of those that a mesh axis runs over, the one named last changes fastest.
Arguments:
- context: bfloat16 [16384, 2048], P('seq'), may hold values from -64 to 64
- wq_cross: bfloat16 [2048, 2048], P(None, 'head'), may hold values from -4 to 4
- wk_cross: bfloat16 [2048, 2048], P(None, 'head'), may hold values from -4 to 4
- wv_cross: bfloat16 [2048, 2048], P(None, 'head'), may hold values from -0.125 to 0.125
- wo_cross: bfloat16 [2048, 2048], P('head'), may hold values from -0.125 to 0.125
- wq_latent: bfloat16 [2048, 2048], P(None, 'head'), may hold values from -4 to 4
- wk_latent: bfloat16 [2048, 2048], P(None, 'head'), may hold values from -4 to 4
- wv_latent: bfloat16 [2048, 2048], P(None, 'head'), may hold values from -0.125 to 0.125
- wo_latent: bfloat16 [2048, 2048], P('head'), may hold values from -0.125 to 0.125
- cross_keep: int32 [16, 2048, 2048], P('head', None, 'seq'), may hold values from 0 to 255, as said below
- latent_keep: int32 [16, 2048, 128], P('head'), may hold values from 0 to 65535, as said below
- residual_keep: int32 [2, 2048, 128], replicated, may hold values from 0 to 65535, as said below
Outputs:
- latents_out: bfloat16 [2048, 2048], P('seq', 'head')
Inputs may be any that keep to these rules, and one draw needn't show every extreme that they name: `cross_keep`: each of the 8 low bits of a word is one keep flag, laid out as the steps say. `latent_keep`: each of the 16 low bits of a word is one keep flag, laid out as the steps say. `residual_keep`: each of the 16 low bits of a word is one keep flag, laid out as the steps say.
All inputs are finite; a program needn't handle non-finite values.
Results may differ from a plain program's by a relative error of at most 0.015.
Values may be sent and summed in bfloat16 or wider, within the bound.
A program may use at most 128 MiB of HBM per device.

v0:
```python
import math
import jax
import jax.numpy as jnp
from jax import lax
from jax.sharding import PartitionSpec as P

keep_scale = 8.0 / 7.0
masked = -1e30


def from_root(value, axis, source):
    kept = jnp.where(lax.axis_index(axis) == source, value, 0).astype(value.dtype)
    return lax.psum(kept, axis)


def unpack_bits(packed_words, word_bits):
    shifts = jnp.arange(word_bits, dtype=jnp.int32)
    bit_table = jnp.bitwise_and(jnp.right_shift(packed_words[..., None, :], shifts[:, None]), 1)
    return bit_table.reshape(packed_words.shape[:-1] + (word_bits * packed_words.shape[-1],))


def rms_rows(matrix):
    wide_rows = matrix.astype(jnp.float32)
    mean_square = jnp.mean(wide_rows * wide_rows, axis=-1, keepdims=True)
    return (wide_rows * lax.rsqrt(mean_square + 1e-06)).astype(jnp.bfloat16)


def per_device(
    context,
    wq_cross,
    wk_cross,
    wv_cross,
    wo_cross,
    wq_latent,
    wk_latent,
    wv_latent,
    wo_latent,
    cross_keep,
    latent_keep,
    residual_keep,
):
    seq_count = lax.axis_size("seq")
    seq_index = lax.axis_index("seq")
    head_index = lax.axis_index("head")
    tok_rows, model_width = context.shape
    head_local = cross_keep.shape[0]
    latent_count = cross_keep.shape[1]
    head_dim = wq_cross.shape[1] // head_local
    query_width = head_local * head_dim
    columns = model_width // lax.axis_size("head")
    local_rows = latent_count // seq_count
    score_scale = 1.0 / math.sqrt(head_dim)
    normed = rms_rows(context)
    key_rows = jnp.dot(normed, wk_cross, preferred_element_type=jnp.float32).astype(jnp.bfloat16)
    value_rows = jnp.dot(normed, wv_cross, preferred_element_type=jnp.float32).astype(jnp.bfloat16)
    own_queries = jnp.dot(normed, wq_cross, preferred_element_type=jnp.float32).astype(jnp.bfloat16)
    own_columns = lax.dynamic_slice_in_dim(context, head_index * columns, columns, 1)
    outgoing_rows = jnp.concatenate([own_queries, own_columns], axis=1)
    arrived_rows = from_root(outgoing_rows, "seq", seq_count - 1)
    queries = arrived_rows[:, :query_width]
    latent_context = arrived_rows[:, query_width:]
    first_latent = (seq_count - 1) * tok_rows
    block_rows = min(512, latent_count)
    block_count = latent_count // block_rows
    query_blocks = queries.reshape(block_count, block_rows, head_local, head_dim)
    mask_blocks = cross_keep.reshape(head_local, block_count, block_rows, -1).transpose(1, 0, 2, 3)
    key_heads = key_rows.reshape(tok_rows, head_local, head_dim)
    value_heads = value_rows.reshape(tok_rows, head_local, head_dim)
    key_pos = seq_index * tok_rows + jnp.arange(tok_rows, dtype=jnp.int32)

    def cross_block(block_items):
        query_block, mask_block, number = block_items
        scores = (
            jnp.einsum("qhd,khd->hqk", query_block, key_heads, preferred_element_type=jnp.float32)
            * score_scale
        )
        query_pos = first_latent + number * block_rows + jnp.arange(block_rows, dtype=jnp.int32)
        allowed = key_pos[None, None, :] <= query_pos[None, :, None]
        scores = jnp.where(allowed, scores, masked)
        row_top = jnp.max(scores, axis=-1)
        exponent = jnp.where(allowed, jnp.exp(scores - row_top[..., None]), 0.0)
        row_sum = jnp.sum(exponent, axis=-1)
        keep_flags = unpack_bits(mask_block, 8).astype(jnp.float32)
        weights = (exponent * keep_flags * keep_scale).astype(jnp.bfloat16)
        summed = jnp.einsum(
            "hqk,khd->hqd", weights, value_heads, preferred_element_type=jnp.float32
        )
        return (summed, row_top, row_sum)

    summed, row_top, row_sum = lax.map(
        cross_block, (query_blocks, mask_blocks, jnp.arange(block_count, dtype=jnp.int32))
    )
    summed = summed.transpose(1, 0, 2, 3).reshape(head_local, latent_count, head_dim)
    row_top = row_top.transpose(1, 0, 2).reshape(head_local, latent_count)
    row_sum = row_sum.transpose(1, 0, 2).reshape(head_local, latent_count)
    first_row = seq_index * local_rows
    row_peak = lax.pmax(row_top, "seq")
    factor = jnp.exp(row_top - row_peak)
    numerator, denominator = (
        lax.psum_scatter(
            (summed * factor[..., None]).astype(jnp.bfloat16),
            "seq",
            scatter_dimension=1,
            tiled=True,
        ).astype(jnp.float32),
        lax.psum_scatter(
            (row_sum * factor).astype(jnp.bfloat16), "seq", scatter_dimension=1, tiled=True
        ).astype(jnp.float32),
    )
    attended_heads = numerator / denominator[..., None]
    attended = (
        attended_heads.transpose(1, 0, 2)
        .reshape(local_rows, head_local * head_dim)
        .astype(jnp.bfloat16)
    )
    inputs = lax.dynamic_slice_in_dim(latent_context, first_row, local_rows, 0).astype(jnp.float32)
    residual_rows = lax.dynamic_slice_in_dim(residual_keep, first_row, local_rows, 1)
    residual_mask = lax.dynamic_slice_in_dim(
        unpack_bits(residual_rows, 16), head_index * columns, columns, 2
    ).astype(jnp.float32)
    branch = jnp.dot(attended, wo_cross, preferred_element_type=jnp.float32)
    branch = lax.psum_scatter(
        branch.astype(jnp.bfloat16), "head", scatter_dimension=1, tiled=True
    ).astype(jnp.float32)
    latents = (inputs + residual_mask[0] * keep_scale * branch).astype(jnp.bfloat16)
    wide_latents = latents.astype(jnp.float32)
    squares = lax.psum(jnp.sum(wide_latents * wide_latents, axis=-1), "head")
    normed_columns = (wide_latents * lax.rsqrt(squares / model_width + 1e-06)[:, None]).astype(
        jnp.bfloat16
    )
    normed_latents = lax.all_gather(normed_columns, "head", axis=1, tiled=True)
    latent_queries = jnp.dot(normed_latents, wq_latent, preferred_element_type=jnp.float32).astype(
        jnp.bfloat16
    )
    latent_keys = jnp.dot(normed_latents, wk_latent, preferred_element_type=jnp.float32).astype(
        jnp.bfloat16
    )
    latent_values = jnp.dot(normed_latents, wv_latent, preferred_element_type=jnp.float32).astype(
        jnp.bfloat16
    )
    my_index = first_row + jnp.arange(local_rows, dtype=jnp.int32)
    latent_words = lax.dynamic_slice_in_dim(latent_keep, first_row, local_rows, 1)
    latent_mask = unpack_bits(latent_words, 16).astype(jnp.float32)
    query_heads = latent_queries.reshape(local_rows, head_local, head_dim)
    initial = (
        jnp.zeros((head_local, local_rows, head_dim), jnp.float32),
        jnp.full((head_local, local_rows), masked, jnp.float32),
        jnp.zeros((head_local, local_rows), jnp.float32),
    )
    key_piece = lax.all_gather(latent_keys, "seq", axis=0, tiled=True)
    value_piece = lax.all_gather(latent_values, "seq", axis=0, tiled=True)
    piece_rows = key_piece.shape[0]
    key_index = jnp.arange(piece_rows, dtype=jnp.int32)

    def update(current):
        weighted, old_top, old_sum = current
        scores = (
            jnp.einsum(
                "qhd,khd->hqk",
                query_heads,
                key_piece.reshape(piece_rows, head_local, head_dim),
                preferred_element_type=jnp.float32,
            )
            * score_scale
        )
        allowed = key_index[None, None, :] <= my_index[None, :, None]
        scores = jnp.where(allowed, scores, masked)
        new_top = jnp.maximum(old_top, jnp.max(scores, axis=-1))
        exponent = jnp.where(allowed, jnp.exp(scores - new_top[..., None]), 0.0)
        keep_flags = jnp.take(latent_mask, key_index, axis=2)
        weights = (exponent * keep_flags * keep_scale).astype(jnp.bfloat16)
        added = jnp.einsum(
            "hqk,khd->hqd",
            weights,
            value_piece.reshape(piece_rows, head_local, head_dim),
            preferred_element_type=jnp.float32,
        )
        return (added, new_top, jnp.sum(exponent, axis=-1))

    needed = jnp.min(key_index) <= jnp.max(my_index)
    weighted, latent_top, latent_sum = lax.cond(needed, update, lambda current: current, initial)
    latent_attended = (
        (weighted / latent_sum[..., None])
        .transpose(1, 0, 2)
        .reshape(local_rows, head_local * head_dim)
        .astype(jnp.bfloat16)
    )
    latent_branch = jnp.dot(latent_attended, wo_latent, preferred_element_type=jnp.float32)
    latent_branch = lax.psum_scatter(
        latent_branch.astype(jnp.bfloat16), "head", scatter_dimension=1, tiled=True
    ).astype(jnp.float32)
    result = (wide_latents + residual_mask[1] * keep_scale * latent_branch).astype(jnp.bfloat16)
    return result


def solution(mesh):
    in_specs = (
        P("seq", None),
        P(None, "head"),
        P(None, "head"),
        P(None, "head"),
        P("head", None),
        P(None, "head"),
        P(None, "head"),
        P(None, "head"),
        P("head", None),
        P("head", None, "seq"),
        P("head", None, None),
        P(),
    )
    out_specs = P("seq", "head")
    return jax.shard_map(
        per_device, mesh=mesh, in_specs=in_specs, out_specs=out_specs, check_vma=False
    )
```

profile of v0, /device:TPU:0, one launch (start us, length us, event | category | flops | bytes accessed | tf_op | source)
XLA Modules:
  0.0 868.4 jit_solution(609139487656249483)
XLA Ops:
  6.5 5.2 fusion.38
  14.8 4.0 copy.67
  18.8 9.7 %convolution_convert_fusion.2 = bf16[2048,512]{0,1:T(8,128)(2,1)} fusion(bf16[2048,512]{1,0:T(8,128)(2,1)S(1)} %copy-done, bf16[2048,2048]{1,0:T(8,128)(2,1)} %param.16, f32[2048]{0:T(1024)S(1)} %add_rsqrt_fusion), kind=kOutput, calls=%fused_computation.67 | convolution fusion | flops 4308598784 | bytes 12591104 | tf_op jit(solution)/shard_map/dot_general | solution.py:56
  28.5 4.1 maximum_select_fusion
  33.1 9.0 %convolution_convert_fusion.1 = bf16[2048,512]{0,1:T(8,128)(2,1)S(1)} fusion(bf16[2048,512]{1,0:T(8,128)(2,1)} %param.18, bf16[2048,2048]{1,0:T(8,128)(2,1)} %param.16, f32[2048]{0:T(1024)S(1)} %add_rsqrt_fusion), kind=kOutput, calls=%fused_computation.66 | convolution fusion | flops 4308598784 | bytes 12591104 | tf_op jit(solution)/shard_map/dot_general | solution.py:54
  44.6 9.0 %convolution_convert_fusion = bf16[2048,512]{0,1:T(8,128)(2,1)S(1)} fusion(bf16[2048,512]{1,0:T(8,128)(2,1)} %param.19, bf16[2048,2048]{1,0:T(8,128)(2,1)} %param.16, f32[2048]{0:T(1024)S(1)} %add_rsqrt_fusion), kind=kOutput, calls=%fused_computation.65 | convolution fusion | flops 4308598784 | bytes 12591104 | tf_op jit(solution)/shard_map/dot_general | solution.py:55
  56.1 135.7 %all-reduce.2.cloned.1.call-done = bf16[2048,1024]{0,1:T(8,128)(2,1)} async-done(((bf16[2048,1024]{0,1:T(8,128)(2,1)}), bf16[2048,1024]{0,1:T(8,128)(2,1)}) %all-reduce.2.cloned.1.call-update) | async-done | bytes 4194320 | tf_op jit(solution)/shard_map/psum | solution.py:13
  191.8 4.8 fusion.60
  196.6 3.3 reshape.146
  202.9 254.1 %while.15 = (s32[]{:T(128)}, f32[4,4,512,128]{3,2,0,1:T(8,128)}, f32[4,4,512]{2,1,0:T(4,128)S(1)}, f32[4,4,512]{2,1,0:T(4,128)S(1)}, s32[4]{0:T(128)S(1)}, /*ind...) while((s32[]{:T(128)}, f32[4,4,512,128]{3,2,0,1:T(8,128)}, ...), condition=%wide.region_5.6_spmd.clone, body=%wide.region_2.5_spmd.clone.sunk | while | flops 2224028160 | bytes 142201040 | solution.py:90
  204.8 7.1 shift_right_arithmetic.115
  211.9 18.0 %shift_right_arithmetic.116 = s32[4,512,2048]{2,1,0:T(8,128)} reshape(s32[4,512,8,256]{3,2,1,0:T(8,128)} %shift_right_arithmetic.115) | data formatting | bytes 33554432 | tf_op jit(solution)/shard_map/while/body/eval_jaxpr/shift_right_arithmetic | solution.py:18
  231.7 10.9 %fusion.86 = (f32[4,512]{1,0:T(4,128)S(1)}, f32[4,512,2048]{2,1,0:T(8,128)}) fusion(pred[512,2048]{1,0:T(8,128)(4,1)S(1)} %broadcast_compare_fusion.3, bf16[2048,4,128]{2,0,1:T(8,128)(2,1)} %get-tuple-element.276, bf16[4,512,4,128]{3,1,2,0:T(8,128)(2,1)} %get-tuple-element.275, s32[]{:T(128)S(6)} %copy.100), kind=kOutput, calls=%fused_computation.33.clone.1 | convolution fusion | flops 1086322688 | bytes 20455428 | tf_op jit(solution)/shard_map/while/body/eval_jaxpr/qhd,khd->hqk/dot_general | solution.py:74
  242.7 15.4 %fusion.87 = f32[4,4,512,128]{3,2,0,1:T(8,128)} fusion(f32[4,4,512,128]{3,2,0,1:T(8,128)} %get-tuple-element.258, s32[]{:T(128)S(6)} %copy.100, bf16[2048,4,128]{2,0,1:T(8,128)(2,1)S(1)} %copy-done.3, s32[4,512,2048]{2,1,0:T(8,128)} %shift_right_arithmetic.116, f32[4,512,2048]{2,1,0:T(8,128)} %get-tuple-element.240, s32[2048]{0:T(1024)S(1)} %bitcast.148, ...), kind=kOutput, calls=%fused_computation.40.clone.1 | convolution fusion | flops 1115684864 | bytes 37765124 | tf_op jit(solution)/shard_map/while/body/eval_jaxpr/hqk,khd->hqd/dot_general | solution.py:85
  258.1 8.4 fusion.88
  268.2 7.1 shift_right_arithmetic.115
  275.3 18.0 %shift_right_arithmetic.116 = s32[4,512,2048]{2,1,0:T(8,128)} reshape(s32[4,512,8,256]{3,2,1,0:T(8,128)} %shift_right_arithmetic.115) | data formatting | bytes 33554432 | tf_op jit(solution)/shard_map/while/body/eval_jaxpr/shift_right_arithmetic | solution.py:18
  295.2 10.9 %fusion.86 = (f32[4,512]{1,0:T(4,128)S(1)}, f32[4,512,2048]{2,1,0:T(8,128)}) fusion(pred[512,2048]{1,0:T(8,128)(4,1)S(1)} %broadcast_compare_fusion.3, bf16[2048,4,128]{2,0,1:T(8,128)(2,1)} %get-tuple-element.276, bf16[4,512,4,128]{3,1,2,0:T(8,128)(2,1)} %get-tuple-element.275, s32[]{:T(128)S(6)} %copy.100), kind=kOutput, calls=%fused_computation.33.clone.1 | convolution fusion | flops 1086322688 | bytes 20455428 | tf_op jit(solution)/shard_map/while/body/eval_jaxpr/qhd,khd->hqk/dot_general | solution.py:74
  306.1 15.5 %fusion.87 = f32[4,4,512,128]{3,2,0,1:T(8,128)} fusion(f32[4,4,512,128]{3,2,0,1:T(8,128)} %get-tuple-element.258, s32[]{:T(128)S(6)} %copy.100, bf16[2048,4,128]{2,0,1:T(8,128)(2,1)S(1)} %copy-done.3, s32[4,512,2048]{2,1,0:T(8,128)} %shift_right_arithmetic.116, f32[4,512,2048]{2,1,0:T(8,128)} %get-tuple-element.240, s32[2048]{0:T(1024)S(1)} %bitcast.148, ...), kind=kOutput, calls=%fused_computation.40.clone.1 | convolution fusion | flops 1115684864 | bytes 37765124 | tf_op jit(solution)/shard_map/while/body/eval_jaxpr/hqk,khd->hqd/dot_general | solution.py:85
  321.6 8.4 fusion.88
  331.7 7.1 shift_right_arithmetic.115
  338.9 18.0 %shift_right_arithmetic.116 = s32[4,512,2048]{2,1,0:T(8,128)} reshape(s32[4,512,8,256]{3,2,1,0:T(8,128)} %shift_right_arithmetic.115) | data formatting | bytes 33554432 | tf_op jit(solution)/shard_map/while/body/eval_jaxpr/shift_right_arithmetic | solution.py:18
  358.7 10.9 %fusion.86 = (f32[4,512]{1,0:T(4,128)S(1)}, f32[4,512,2048]{2,1,0:T(8,128)}) fusion(pred[512,2048]{1,0:T(8,128)(4,1)S(1)} %broadcast_compare_fusion.3, bf16[2048,4,128]{2,0,1:T(8,128)(2,1)} %get-tuple-element.276, bf16[4,512,4,128]{3,1,2,0:T(8,128)(2,1)} %get-tuple-element.275, s32[]{:T(128)S(6)} %copy.100), kind=kOutput, calls=%fused_computation.33.clone.1 | convolution fusion | flops 1086322688 | bytes 20455428 | tf_op jit(solution)/shard_map/while/body/eval_jaxpr/qhd,khd->hqk/dot_general | solution.py:74
  369.7 15.4 %fusion.87 = f32[4,4,512,128]{3,2,0,1:T(8,128)} fusion(f32[4,4,512,128]{3,2,0,1:T(8,128)} %get-tuple-element.258, s32[]{:T(128)S(6)} %copy.100, bf16[2048,4,128]{2,0,1:T(8,128)(2,1)S(1)} %copy-done.3, s32[4,512,2048]{2,1,0:T(8,128)} %shift_right_arithmetic.116, f32[4,512,2048]{2,1,0:T(8,128)} %get-tuple-element.240, s32[2048]{0:T(1024)S(1)} %bitcast.148, ...), kind=kOutput, calls=%fused_computation.40.clone.1 | convolution fusion | flops 1115684864 | bytes 37765124 | tf_op jit(solution)/shard_map/while/body/eval_jaxpr/hqk,khd->hqd/dot_general | solution.py:85
  385.1 8.4 fusion.88
  395.2 7.1 shift_right_arithmetic.115
  402.3 18.0 %shift_right_arithmetic.116 = s32[4,512,2048]{2,1,0:T(8,128)} reshape(s32[4,512,8,256]{3,2,1,0:T(8,128)} %shift_right_arithmetic.115) | data formatting | bytes 33554432 | tf_op jit(solution)/shard_map/while/body/eval_jaxpr/shift_right_arithmetic | solution.py:18
  422.2 10.9 %fusion.86 = (f32[4,512]{1,0:T(4,128)S(1)}, f32[4,512,2048]{2,1,0:T(8,128)}) fusion(pred[512,2048]{1,0:T(8,128)(4,1)S(1)} %broadcast_compare_fusion.3, bf16[2048,4,128]{2,0,1:T(8,128)(2,1)} %get-tuple-element.276, bf16[4,512,4,128]{3,1,2,0:T(8,128)(2,1)} %get-tuple-element.275, s32[]{:T(128)S(6)} %copy.100), kind=kOutput, calls=%fused_computation.33.clone.1 | convolution fusion | flops 1086322688 | bytes 20455428 | tf_op jit(solution)/shard_map/while/body/eval_jaxpr/qhd,khd->hqk/dot_general | solution.py:74
  433.1 15.4 %fusion.87 = f32[4,4,512,128]{3,2,0,1:T(8,128)} fusion(f32[4,4,512,128]{3,2,0,1:T(8,128)} %get-tuple-element.258, s32[]{:T(128)S(6)} %copy.100, bf16[2048,4,128]{2,0,1:T(8,128)(2,1)S(1)} %copy-done.3, s32[4,512,2048]{2,1,0:T(8,128)} %shift_right_arithmetic.116, f32[4,512,2048]{2,1,0:T(8,128)} %get-tuple-element.240, s32[2048]{0:T(1024)S(1)} %bitcast.148, ...), kind=kOutput, calls=%fused_computation.40.clone.1 | convolution fusion | flops 1115684864 | bytes 37765124 | tf_op jit(solution)/shard_map/while/body/eval_jaxpr/hqk,khd->hqd/dot_general | solution.py:85
  448.6 8.4 fusion.88
  457.0 34.9 %pmax.7 = f32[4,2048]{1,0:T(4,128)S(1)} all-reduce(f32[4,2048]{1,0:T(4,128)S(1)} %bitcast.149), channel_id=1, replica_groups=mesh['seq'=8,'head'=4] {'seq'}, use_global_device_ids=true, to_apply=%region_6.7 | all-reduce | flops 8192 | bytes 65536 | tf_op jit(solution)/shard_map/pmax | solution.py:97
  493.0 4.2 fusion.42
  497.2 55.8 %reduce-scatter.13.cloned.1.call-done = bf16[256,4]{1,0:T(8,128)(2,1)} async-done(((bf16[2048,4]{1,0:T(8,128)(2,1)}), bf16[256,4]{1,0:T(8,128)(2,1)}) %reduce-scatter.13.cloned.1.call-update) | async-done | bytes 2064
  553.9 70.6 %reduce-scatter.7.cloned.1.call-done = bf16[4,256,128]{2,1,0:T(8,128)(2,1)} async-done(((bf16[4,2048,128]{2,1,0:T(8,128)(2,1)}), bf16[4,256,128]{2,1,0:T(8,128)(2,1)}) %reduce-scatter.7.cloned.1.call-update) | async-done | bytes 262160 | tf_op jit(solution)/shard_map/reduce_scatter | solution.py:100
  629.8 22.2 %reduce-scatter.9.cloned.1.call-done = bf16[256,512]{0,1:T(8,128)(2,1)} async-done(((bf16[256,2048]{0,1:T(8,128)(2,1)}), bf16[256,512]{0,1:T(8,128)(2,1)}) %reduce-scatter.9.cloned.1.call-update) | async-done | bytes 262160 | tf_op jit(solution)/shard_map/reduce_scatter | solution.py:122
  653.1 5.8 psum.15
  659.7 17.4 %all-gather.4.cloned.1.call-done = bf16[256,2048]{0,1:T(8,128)(2,1)} async-done(((bf16[256,512]{0,1:T(8,128)(2,1)}), bf16[256,2048]{0,1:T(8,128)(2,1)}) %all-gather.4.cloned.1.call-update) | async-done | bytes 1048592 | tf_op jit(solution)/shard_map/all_gather | solution.py:131
  677.1 3.4 convolution_convert_fusion.6
  686.5 7.2 fusion.41
  694.4 35.4 %all-gather.6.cloned.1.call-done = bf16[2048,512]{1,0:T(8,128)(2,1)} async-done(((bf16[256,512]{1,0:T(8,128)(2,1)}), bf16[2048,512]{1,0:T(8,128)(2,1)}) %all-gather.6.cloned.1.call-update) | async-done | bytes 2097168 | tf_op jit(solution)/shard_map/all_gather | solution.py:150
  729.8 49.8 %all-gather.8.cloned.1.call-done = bf16[2048,512]{1,0:T(8,128)(2,1)} async-done(((bf16[256,512]{1,0:T(8,128)(2,1)}), bf16[2048,512]{1,0:T(8,128)(2,1)}) %all-gather.8.cloned.1.call-update) | async-done | bytes 2097168 | tf_op jit(solution)/shard_map/all_gather | solution.py:151
  779.6 49.9 %conditional.1 = (f32[4,256]{1,0:T(4,128)S(1)}, f32[4,256,128]{1,2,0:T(8,128)}) conditional(s32[]{:T(128)} %convert_element_type.119, () %tuple.18, (s32[2048]{0:T(1024)S(1)}, s32[256]{0:T(256)S(1)}, bf16[256,512]{1,0:T(8,128)(2,1)S(1)}, bf16[2048,512]{1,0:T(8,128)(2,1)}, s32[2048]{0:T(1024)S(1)}, /*index=5*/s32[2048]{0:T(1024)S(1)}, ...), branch_computations={%region_13.14_spmd, %region_14.17_spmd} | conditional | flops 1107840000 | bytes 107811880 | solution.py:181
  780.0 3.5 fusion.4
  786.7 22.2 %gather_fusion = f32[2048,4,256]{2,1,0:T(4,128)} fusion(f32[4,256,2048]{1,0,2:T(4,128)} %get-tuple-element.76, s32[2048]{0:T(1024)S(1)} %fusion.17), kind=kCustom, calls=%fused_computation | custom fusion | bytes 16785408 | tf_op jit(solution)/shard_map/cond/branch_1_fun/jit(_take)/gather | solution.py:170
  808.9 9.9 %copy.43 = f32[2048,4,256]{0,2,1:T(8,128)} copy(f32[2048,4,256]{2,1,0:T(4,128)} %gather_fusion) | data formatting | bytes 16777216 | tf_op jit(solution)/shard_map/cond/branch_1_fun/jit(_take)/gather | solution.py:170
  818.8 10.7 %fusion.6 = f32[4,256,128]{1,2,0:T(8,128)} fusion(f32[2048,4,256]{0,2,1:T(8,128)} %copy.43, f32[4,256,2048]{2,1,0:T(8,128)} %copy-done.2, f32[4,256]{1,0:T(4,128)S(1)} %broadcast_maximum_fusion, pred[2048]{0:T(1024)(128)(4,1)S(1)} %compare_and_fusion, pred[256,2048]{1,0:T(8,128)(4,1)S(1)} %broadcast_compare_fusion, bf16[2048,512]{1,0:T(8,128)(2,1)} %get-tuple-element.78), kind=kOutput, calls=%fused_computation.9 | convolution fusion | flops 553648128 | bytes 19929088 | tf_op jit(solution)/shard_map/cond | solution.py:181
  830.8 3.5 convolution_convert_fusion.3
  834.3 23.5 %reduce-scatter.11.cloned.1.call-done = bf16[256,512]{0,1:T(8,128)(2,1)} async-done(((bf16[256,2048]{0,1:T(8,128)(2,1)}), bf16[256,512]{0,1:T(8,128)(2,1)}) %reduce-scatter.11.cloned.1.call-update) | async-done | bytes 262160 | tf_op jit(solution)/shard_map/reduce_scatter | solution.py:189
  (110 shorter events, 47.0 us)
Async XLA Ops:
  6.5 12.2 %copy-start = (bf16[2048,512]{1,0:T(8,128)(2,1)S(1)}, bf16[2048,512]{1,0:T(8,128)(2,1)}, u32[]{:S(2)}) copy-start(bf16[2048,512]{1,0:T(8,128)(2,1)} %param.17) | copy-start | bytes 6291460
  6.5 185.3 %all-reduce.2.cloned.1.call-start = ((), (), s32[]{:S(2)}) async-start(), calls=%async_computation.4 | async-start | bytes 8388608 | tf_op jit(solution)/shard_map/psum | solution.py:13
  32.6 520.4 %reduce-scatter.13.cloned.1.call-start = ((), (), s32[]{:S(2)}) async-start(), calls=%async_computation.11 | async-start | bytes 589824
  231.7 11.0 %copy-start.3 = (bf16[2048,4,128]{2,0,1:T(8,128)(2,1)S(1)}, bf16[2048,4,128]{2,0,1:T(8,128)(2,1)}, u32[]{:S(2)}) copy-start(bf16[2048,4,128]{2,0,1:T(8,128)(2,1)} %get-tuple-element.278) | copy-start | bytes 6291460 | tf_op jit(solution)/shard_map/while
  295.2 11.0 %copy-start.3 = (bf16[2048,4,128]{2,0,1:T(8,128)(2,1)S(1)}, bf16[2048,4,128]{2,0,1:T(8,128)(2,1)}, u32[]{:S(2)}) copy-start(bf16[2048,4,128]{2,0,1:T(8,128)(2,1)} %get-tuple-element.278) | copy-start | bytes 6291460 | tf_op jit(solution)/shard_map/while
  358.7 11.0 %copy-start.3 = (bf16[2048,4,128]{2,0,1:T(8,128)(2,1)S(1)}, bf16[2048,4,128]{2,0,1:T(8,128)(2,1)}, u32[]{:S(2)}) copy-start(bf16[2048,4,128]{2,0,1:T(8,128)(2,1)} %get-tuple-element.278) | copy-start | bytes 6291460 | tf_op jit(solution)/shard_map/while
  422.2 11.0 %copy-start.3 = (bf16[2048,4,128]{2,0,1:T(8,128)(2,1)S(1)}, bf16[2048,4,128]{2,0,1:T(8,128)(2,1)}, u32[]{:S(2)}) copy-start(bf16[2048,4,128]{2,0,1:T(8,128)(2,1)} %get-tuple-element.278) | copy-start | bytes 6291460 | tf_op jit(solution)/shard_map/while
  492.9 131.6 %reduce-scatter.7.cloned.1.call-start = ((), (), s32[]{:S(2)}) async-start(), calls=%async_computation.5 | async-start | bytes 2359296 | tf_op jit(solution)/shard_map/reduce_scatter | solution.py:100
  493.0 132.9 %copy-start.4 = (bf16[512,2048]{1,0:T(8,128)(2,1)S(1)}, bf16[512,2048]{1,0:T(8,128)(2,1)}, u32[]{:S(2)}) copy-start(bf16[512,2048]{1,0:T(8,128)(2,1)} %param.20) | copy-start | bytes 6291460
  497.2 154.7 %reduce-scatter.9.cloned.1.call-start = ((), (), s32[]{:S(2)}) async-start(), calls=%async_computation.6 | async-start | bytes 1310720 | tf_op jit(solution)/shard_map/reduce_scatter | solution.py:122
  627.9 49.3 %all-gather.4.cloned.1.call-start = ((), (), s32[]{:S(2)}) async-start(), calls=%async_computation.7 | async-start | bytes 1310720 | tf_op jit(solution)/shard_map/all_gather | solution.py:131
  659.7 70.2 %all-gather.6.cloned.1.call-start = ((), (), s32[]{:S(2)}) async-start(), calls=%async_computation.8 | async-start | bytes 2359296 | tf_op jit(solution)/shard_map/all_gather | solution.py:150
  677.1 3.5 copy-start.6
  680.6 99.0 %all-gather.8.cloned.1.call-start = ((), (), s32[]{:S(2)}) async-start(), calls=%async_computation.9 | async-start | bytes 2359296 | tf_op jit(solution)/shard_map/all_gather | solution.py:151
  683.7 174.1 %reduce-scatter.11.cloned.1.call-start = ((), (), s32[]{:S(2)}) async-start(), calls=%async_computation.10 | async-start | bytes 1310720 | tf_op jit(solution)/shard_map/reduce_scatter | solution.py:189
  686.5 7.2 copy-start.5
  686.5 7.2 copy-start.7
  783.5 3.2 copy-start.2
  829.5 31.8 %copy-start.1 = (bf16[2048,512]{1,0:T(8,128)(2,1)S(1)}, bf16[2048,512]{1,0:T(8,128)(2,1)}, u32[]{:S(2)}) copy-start(bf16[2048,512]{1,0:T(8,128)(2,1)} %param.17) | copy-start | bytes 6291460
Sparse Core Ops, SparseCore 0:
  32.7 159.0 all-reduce.1
  493.1 59.9 reduce-scatter.12
  556.6 67.9 reduce-scatter.6
  628.0 23.9 reduce-scatter.8
  659.8 17.3 all-gather.3
  680.7 49.0 all-gather.5
  732.0 47.6 all-gather.7
  834.4 23.3 reduce-scatter.10
where the time goes:
time: 877 us; the launch traced here: 868 us
  waiting for transfers between devices  411 us (47%)
  local copies, waits for them, and re-layouts  173 us (20%)
  matrix products  160 us (18%)
  other arithmetic  66.6 us (8%)
  blocking collectives  40.6 us (5%)
  between operations  14.6 us (2%)
    psum x1, waiting for transfers between devices, from_root(): return lax.psum(kept, axis)  136 us
    shift_right_arithmetic x14, local copies, waits for them, and re-layouts, unpack_bits(): jnp.right_shift(packed_words[..., None, :], shifts[:, None])  108 us
    reduce_scatter x1, waiting for transfers between devices, per_device(): lax.psum_scatter((summed * factor[..., None]).astype(jnp.bfloat16), 'seq'...  70.6 us
    dot_general x4, matrix products, cross_block(): jnp.einsum('hqk,khd->hqd', weights, value_heads, preferred_element_type=j...  61.8 us
    unnamed x9, waiting for transfers between devices  55.9 us
    all_gather x1, waiting for transfers between devices, per_device(): value_piece = lax.all_gather(latent_values, 'seq', axis=0, tiled=True)  49.8 us
    dot_general x4, matrix products, cross_block(): jnp.einsum('qhd,khd->hqk', query_block, key_heads, preferred_element_type...  43.7 us
    all_gather x1, waiting for transfers between devices, per_device(): key_piece = lax.all_gather(latent_keys, 'seq', axis=0, tiled=True)  35.4 us
  transfers between devices with their start and end apart: 8, of which 8 were waited for; matrix products, arithmetic and copies ran while one was open for 5% of the time, Pallas kernels for 0%

commit v1 on v0

--- a/solution.py
+++ b/solution.py
@@ -10,7 +10,7 @@
 
 def from_root(value, axis, source):
     kept = jnp.where(lax.axis_index(axis) == source, value, 0).astype(value.dtype)
-    return lax.psum(kept, axis)
+    return jnp.sum(lax.all_gather(kept, axis), axis=0)
 
 
 def unpack_bits(packed_words, word_bits):

time: 877 us -> 1370 us (1.56)
  waiting for transfers between devices: 411 us -> 883 us
  other arithmetic: 66.6 us -> 81.9 us
    all_gather x0 -> x1, waiting for transfers between devices: none -> 616 us  [from_root(): return jnp.sum(lax.all_gather(kept, axis), axis=0)]
    psum x1 -> x0, waiting for transfers between devices: 136 us -> none  [from_root(): return lax.psum(kept, axis)]
    reduce_sum x0 -> x1, other arithmetic: none -> 14.1 us  [from_root(): return jnp.sum(lax.all_gather(kept, axis), axis=0)]
    shift_right_arithmetic x14 -> x15, local copies, waits for them, and re-layouts: 108 us -> 115 us  [unpack_bits(): jnp.right_shift(packed_words[..., None, :], shifts[:, None])]
  transfers between devices with their start and end apart: 8 -> 8, of which waited for: 8 -> 8; matrix products, arithmetic and copies ran while one was open for 5% -> 4% of each run, Pallas kernels for 0% -> 0%
where the time goes in v1:
time: 1370 us; the launch traced here: 1360 us
  waiting for transfers between devices  883 us (64%)
  local copies, waits for them, and re-layouts  184 us (13%)
  matrix products  154 us (11%)
  other arithmetic  81.9 us (6%)
  blocking collectives  41.7 us (3%)
  between operations  14.6 us (1%)
    all_gather x1, waiting for transfers between devices, from_root(): return jnp.sum(lax.all_gather(kept, axis), axis=0)  616 us
    shift_right_arithmetic x15, local copies, waits for them, and re-layouts, unpack_bits(): jnp.right_shift(packed_words[..., None, :], shifts[:, None])  115 us
    reduce_scatter x1, waiting for transfers between devices, per_device(): lax.psum_scatter((summed * factor[..., None]).astype(jnp.bfloat16), 'seq'...  70.5 us
    dot_general x4, matrix products, cross_block(): jnp.einsum('hqk,khd->hqd', weights, value_heads, preferred_element_type=j...  61.8 us
    unnamed x9, waiting for transfers between devices  56.3 us
    all_gather x1, waiting for transfers between devices, per_device(): value_piece = lax.all_gather(latent_values, 'seq', axis=0, tiled=True)  49.8 us
    dot_general x4, matrix products, cross_block(): jnp.einsum('qhd,khd->hqk', query_block, key_heads, preferred_element_type...  37.4 us
    pmax x1, blocking collectives, per_device(): row_peak = lax.pmax(row_top, 'seq')  36 us
  transfers between devices with their start and end apart: 8, of which 8 were waited for; matrix products, arithmetic and copies ran while one was open for 4% of the time, Pallas kernels for 0%

profile of v1, /device:TPU:0, one launch (start us, length us, event | category | flops | bytes accessed | tf_op | source)
XLA Modules:
  0.0 1363.0 jit_solution(18334447205237048901)
XLA Ops:
  6.5 5.2 fusion.35
  14.9 3.9 copy.37
  18.8 9.7 fusion.40
  28.5 4.1 maximum_select_fusion
  32.6 6.4 copy.38
  39.4 9.0 convolution_convert_fusion.1
  51.4 9.3 convolution_convert_fusion
  63.2 616.3 %all-gather.5.cloned.1.call-done = bf16[8,2048,1024]{2,1,0:T(8,128)(2,1)} async-done(((bf16[1,2048,1024]{2,1,0:T(8,128)(2,1)}), bf16[8,2048,1024]{2,1,0:T(8,128)(2,1)}) %all-gather.5.cloned.1.call-update) | async-done | bytes 33554448 | tf_op jit(solution)/shard_map/all_gather | solution.py:13
  679.5 14.1 %reduce_sum.49 = bf16[2048,1024]{1,0:T(8,128)(2,1)} reduce(bf16[8,2048,1024]{2,1,0:T(8,128)(2,1)} %all-gather.5.cloned.1.call-done, bf16[]{:T(256)} %constant.99.clone.1), dimensions={0}, to_apply=%region_1.2 | reduce | flops 14680064 | bytes 37748736 | tf_op jit(solution)/shard_map/reduce_sum | solution.py:13
  693.7 3.8 fusion.58
  699.5 253.0 %while.15 = (s32[]{:T(128)}, f32[4,4,512,128]{3,2,0,1:T(8,128)}, f32[4,4,512]{2,1,0:T(4,128)S(1)}, f32[4,4,512]{2,1,0:T(4,128)S(1)}, s32[4]{0:T(128)S(1)}, /*ind...) while((s32[]{:T(128)}, f32[4,4,512,128]{3,2,0,1:T(8,128)}, ...), condition=%wide.region_5.6_spmd.clone, body=%wide.region_2.5_spmd.clone.sunk | while | flops 2224028160 | bytes 143249616 | solution.py:90
  701.4 7.1 shift_right_arithmetic.115
  708.5 18.0 %shift_right_arithmetic.116 = s32[4,512,2048]{2,1,0:T(8,128)} reshape(s32[4,512,8,256]{3,2,1,0:T(8,128)} %shift_right_arithmetic.115) | data formatting | bytes 33554432 | tf_op jit(solution)/shard_map/while/body/eval_jaxpr/shift_right_arithmetic | solution.py:18
  729.7 9.3 fusion.84
  739.0 15.4 %fusion.85 = f32[4,4,512,128]{3,2,0,1:T(8,128)} fusion(f32[4,4,512,128]{3,2,0,1:T(8,128)} %get-tuple-element.258, s32[]{:T(128)S(6)} %copy.102, bf16[2048,4,128]{2,0,1:T(8,128)(2,1)S(1)} %copy-done.3, s32[4,512,2048]{2,1,0:T(8,128)} %shift_right_arithmetic.116, f32[4,512,2048]{2,1,0:T(8,128)} %get-tuple-element.240, s32[2048]{0:T(1024)S(1)} %bitcast.150, ...), kind=kOutput, calls=%fused_computation.40.clone.1 | convolution fusion | flops 1115684864 | bytes 37765124 | tf_op jit(solution)/shard_map/while/body/eval_jaxpr/hqk,khd->hqd/dot_general | solution.py:85
  754.5 8.4 fusion.86
  764.6 7.1 shift_right_arithmetic.115
  771.7 18.0 %shift_right_arithmetic.116 = s32[4,512,2048]{2,1,0:T(8,128)} reshape(s32[4,512,8,256]{3,2,1,0:T(8,128)} %shift_right_arithmetic.115) | data formatting | bytes 33554432 | tf_op jit(solution)/shard_map/while/body/eval_jaxpr/shift_right_arithmetic | solution.py:18
  792.9 9.3 fusion.84
  802.2 15.5 %fusion.85 = f32[4,4,512,128]{3,2,0,1:T(8,128)} fusion(f32[4,4,512,128]{3,2,0,1:T(8,128)} %get-tuple-element.258, s32[]{:T(128)S(6)} %copy.102, bf16[2048,4,128]{2,0,1:T(8,128)(2,1)S(1)} %copy-done.3, s32[4,512,2048]{2,1,0:T(8,128)} %shift_right_arithmetic.116, f32[4,512,2048]{2,1,0:T(8,128)} %get-tuple-element.240, s32[2048]{0:T(1024)S(1)} %bitcast.150, ...), kind=kOutput, calls=%fused_computation.40.clone.1 | convolution fusion | flops 1115684864 | bytes 37765124 | tf_op jit(solution)/shard_map/while/body/eval_jaxpr/hqk,khd->hqd/dot_general | solution.py:85
  817.7 8.4 fusion.86
  827.8 7.1 shift_right_arithmetic.115
  835.0 18.0 %shift_right_arithmetic.116 = s32[4,512,2048]{2,1,0:T(8,128)} reshape(s32[4,512,8,256]{3,2,1,0:T(8,128)} %shift_right_arithmetic.115) | data formatting | bytes 33554432 | tf_op jit(solution)/shard_map/while/body/eval_jaxpr/shift_right_arithmetic | solution.py:18
  856.1 9.4 fusion.84
  865.5 15.4 %fusion.85 = f32[4,4,512,128]{3,2,0,1:T(8,128)} fusion(f32[4,4,512,128]{3,2,0,1:T(8,128)} %get-tuple-element.258, s32[]{:T(128)S(6)} %copy.102, bf16[2048,4,128]{2,0,1:T(8,128)(2,1)S(1)} %copy-done.3, s32[4,512,2048]{2,1,0:T(8,128)} %shift_right_arithmetic.116, f32[4,512,2048]{2,1,0:T(8,128)} %get-tuple-element.240, s32[2048]{0:T(1024)S(1)} %bitcast.150, ...), kind=kOutput, calls=%fused_computation.40.clone.1 | convolution fusion | flops 1115684864 | bytes 37765124 | tf_op jit(solution)/shard_map/while/body/eval_jaxpr/hqk,khd->hqd/dot_general | solution.py:85
  880.9 8.4 fusion.86
  891.0 7.1 shift_right_arithmetic.115
  898.2 18.0 %shift_right_arithmetic.116 = s32[4,512,2048]{2,1,0:T(8,128)} reshape(s32[4,512,8,256]{3,2,1,0:T(8,128)} %shift_right_arithmetic.115) | data formatting | bytes 33554432 | tf_op jit(solution)/shard_map/while/body/eval_jaxpr/shift_right_arithmetic | solution.py:18
  919.3 9.3 fusion.84
  928.7 15.4 %fusion.85 = f32[4,4,512,128]{3,2,0,1:T(8,128)} fusion(f32[4,4,512,128]{3,2,0,1:T(8,128)} %get-tuple-element.258, s32[]{:T(128)S(6)} %copy.102, bf16[2048,4,128]{2,0,1:T(8,128)(2,1)S(1)} %copy-done.3, s32[4,512,2048]{2,1,0:T(8,128)} %shift_right_arithmetic.116, f32[4,512,2048]{2,1,0:T(8,128)} %get-tuple-element.240, s32[2048]{0:T(1024)S(1)} %bitcast.150, ...), kind=kOutput, calls=%fused_computation.40.clone.1 | convolution fusion | flops 1115684864 | bytes 37765124 | tf_op jit(solution)/shard_map/while/body/eval_jaxpr/hqk,khd->hqd/dot_general | solution.py:85
  944.1 8.4 fusion.86
  952.5 36.0 %pmax.7 = f32[4,2048]{1,0:T(4,128)S(1)} all-reduce(f32[4,2048]{1,0:T(4,128)S(1)} %bitcast.151), channel_id=1, replica_groups=mesh['seq'=8,'head'=4] {'seq'}, use_global_device_ids=true, to_apply=%region_6.7 | all-reduce | flops 8192 | bytes 65536 | tf_op jit(solution)/shard_map/pmax | solution.py:97
  989.6 4.0 fusion.39
  993.7 56.1 %reduce-scatter.13.cloned.1.call-done = bf16[256,4]{1,0:T(8,128)(2,1)} async-done(((bf16[2048,4]{1,0:T(8,128)(2,1)}), bf16[256,4]{1,0:T(8,128)(2,1)}) %reduce-scatter.13.cloned.1.call-update) | async-done | bytes 2064
  1050.8 70.5 %reduce-scatter.7.cloned.1.call-done = bf16[4,256,128]{2,1,0:T(8,128)(2,1)} async-done(((bf16[4,2048,128]{2,1,0:T(8,128)(2,1)}), bf16[4,256,128]{2,1,0:T(8,128)(2,1)}) %reduce-scatter.7.cloned.1.call-update) | async-done | bytes 262160 | tf_op jit(solution)/shard_map/reduce_scatter | solution.py:100
  1127.9 5.1 shift_right_arithmetic.63
  1134.4 14.1 %reduce-scatter.9.cloned.1.call-done = bf16[256,512]{1,0:T(8,128)(2,1)} async-done(((bf16[256,2048]{1,0:T(8,128)(2,1)}), bf16[256,512]{1,0:T(8,128)(2,1)}) %reduce-scatter.9.cloned.1.call-update) | async-done | bytes 262160 | tf_op jit(solution)/shard_map/reduce_scatter | solution.py:122
  1149.7 5.8 psum.7
  1156.3 17.4 %all-gather.7.cloned.1.call-done = bf16[256,2048]{1,0:T(8,128)(2,1)} async-done(((bf16[256,512]{1,0:T(8,128)(2,1)}), bf16[256,2048]{1,0:T(8,128)(2,1)}) %all-gather.7.cloned.1.call-update) | async-done | bytes 1048592 | tf_op jit(solution)/shard_map/all_gather | solution.py:131
  1183.3 7.2 fusion.38
  1191.3 35.1 %all-gather.9.cloned.1.call-done = bf16[2048,512]{1,0:T(8,128)(2,1)} async-done(((bf16[256,512]{1,0:T(8,128)(2,1)}), bf16[2048,512]{1,0:T(8,128)(2,1)}) %all-gather.9.cloned.1.call-update) | async-done | bytes 2097168 | tf_op jit(solution)/shard_map/all_gather | solution.py:150
  1226.4 49.8 %all-gather.11.cloned.1.call-done = bf16[2048,512]{1,0:T(8,128)(2,1)} async-done(((bf16[256,512]{1,0:T(8,128)(2,1)}), bf16[2048,512]{1,0:T(8,128)(2,1)}) %all-gather.11.cloned.1.call-update) | async-done | bytes 2097168 | tf_op jit(solution)/shard_map/all_gather | solution.py:151
  1276.1 49.9 %conditional.1 = (f32[4,256]{1,0:T(4,128)S(1)}, f32[4,256,128]{1,2,0:T(8,128)}) conditional(s32[]{:T(128)} %convert_element_type.121, () %tuple.18, (s32[2048]{0:T(1024)S(1)}, s32[256]{0:T(256)S(1)}, bf16[256,512]{1,0:T(8,128)(2,1)S(1)}, bf16[2048,512]{1,0:T(8,128)(2,1)}, s32[2048]{0:T(1024)S(1)}, /*index=5*/s32[2048]{0:T(1024)S(1)}, ...), branch_computations={%region_13.14_spmd, %region_14.17_spmd} | conditional | flops 1107840000 | bytes 107811880 | solution.py:181
  1276.5 3.5 fusion.4
  1283.2 22.2 %gather_fusion = f32[2048,4,256]{2,1,0:T(4,128)} fusion(f32[4,256,2048]{1,0,2:T(4,128)} %get-tuple-element.76, s32[2048]{0:T(1024)S(1)} %fusion.17), kind=kCustom, calls=%fused_computation | custom fusion | bytes 16785408 | tf_op jit(solution)/shard_map/cond/branch_1_fun/jit(_take)/gather | solution.py:170
  1305.4 9.9 copy.35
  1315.4 10.7 fusion.6
  1330.6 23.5 %reduce-scatter.11.cloned.1.call-done = bf16[256,512]{1,0:T(8,128)(2,1)} async-done(((bf16[256,2048]{1,0:T(8,128)(2,1)}), bf16[256,512]{1,0:T(8,128)(2,1)}) %reduce-scatter.11.cloned.1.call-update) | async-done | bytes 262160 | tf_op jit(solution)/shard_map/reduce_scatter | solution.py:189
  (112 shorter events, 59.7 us)
Async XLA Ops:
  6.5 12.3 copy-start
  6.5 673.0 %all-gather.5.cloned.1.call-start = ((), (), s32[]{:S(2)}) async-start(), calls=%async_computation.4 | async-start | bytes 37748736 | tf_op jit(solution)/shard_map/all_gather | solution.py:13
  39.0 1010.8 %reduce-scatter.13.cloned.1.call-start = ((), (), s32[]{:S(2)}) async-start(), calls=%async_computation.11 | async-start | bytes 589824
  729.7 9.4 copy-start.3
  792.9 9.4 copy-start.3
  856.1 9.4 copy-start.3
  919.3 9.4 copy-start.3
  989.6 131.7 %reduce-scatter.7.cloned.1.call-start = ((), (), s32[]{:S(2)}) async-start(), calls=%async_computation.5 | async-start | bytes 2359296 | tf_op jit(solution)/shard_map/reduce_scatter | solution.py:100
  989.6 132.9 %copy-start.4 = (bf16[512,2048]{1,0:T(8,128)(2,1)S(1)}, bf16[512,2048]{1,0:T(8,128)(2,1)}, u32[]{:S(2)}) copy-start(bf16[512,2048]{1,0:T(8,128)(2,1)} %param.20) | copy-start | bytes 6291460
  993.7 154.8 %reduce-scatter.9.cloned.1.call-start = ((), (), s32[]{:S(2)}) async-start(), calls=%async_computation.6 | async-start | bytes 1310720 | tf_op jit(solution)/shard_map/reduce_scatter | solution.py:122
  1124.4 49.4 %all-gather.7.cloned.1.call-start = ((), (), s32[]{:S(2)}) async-start(), calls=%async_computation.7 | async-start | bytes 1310720 | tf_op jit(solution)/shard_map/all_gather | solution.py:131
  1156.3 70.1 %all-gather.9.cloned.1.call-start = ((), (), s32[]{:S(2)}) async-start(), calls=%async_computation.8 | async-start | bytes 2359296 | tf_op jit(solution)/shard_map/all_gather | solution.py:150
  1177.1 99.0 %all-gather.11.cloned.1.call-start = ((), (), s32[]{:S(2)}) async-start(), calls=%async_computation.9 | async-start | bytes 2359296 | tf_op jit(solution)/shard_map/all_gather | solution.py:151
  1180.5 173.6 %reduce-scatter.11.cloned.1.call-start = ((), (), s32[]{:S(2)}) async-start(), calls=%async_computation.10 | async-start | bytes 1310720 | tf_op jit(solution)/shard_map/reduce_scatter | solution.py:189
  1183.3 7.2 copy-start.5
  1183.3 7.2 copy-start.6
  1280.0 3.2 copy-start.2
  1326.1 29.8 %copy-start.1 = (bf16[2048,512]{1,0:T(8,128)(2,1)S(1)}, bf16[2048,512]{1,0:T(8,128)(2,1)}, u32[]{:S(2)}) copy-start(bf16[2048,512]{1,0:T(8,128)(2,1)} %param.17) | copy-start | bytes 6291460
Sparse Core Ops, SparseCore 0:
  39.1 640.3 all-gather.4
  989.7 60.1 reduce-scatter.12
  1053.4 67.8 reduce-scatter.6
  1124.5 23.8 reduce-scatter.8
  1156.4 17.3 all-gather.6
  1177.2 49.0 all-gather.8
  1228.5 47.6 all-gather.10
  1330.8 23.3 reduce-scatter.10
